TPU v7x, 32 devices: a whole 2x2x4 slice. The times are simulated.
32 devices in a mesh: narrow: 4 (over y, x), region: 8 (over z, core).
Axes of the slice: x: 2, y: 2, z: 4, core: 2. Of those that a mesh axis runs over, the one named last changes fastest.
Arguments:
- point_feats: bfloat16 [64, 131072], P(None, ('narrow', 'region')), may hold values from -6 to 6
- point_owner: int32 [131072, 1], P(('narrow', 'region')), may hold values from 0 to 31; in each aligned block of 4096 rows (0 to 4095, 4096 to 8191, ...) at most 256 rows name the same one
- point_voxel: int32 [131072], P(('narrow', 'region')), may hold values from 0 to 12287
- weight: bfloat16 [9, 64, 192], replicated, may hold values from -0.15625 to 0.15625
- cotangent: bfloat16 [64, 192, 2048], P(None, 'region', 'narrow'), may hold values from -6 to 6
Outputs:
- conv_out: bfloat16 [64, 192, 2048], P(None, 'region', 'narrow')
- point_grad: bfloat16 [64, 131072], P(None, ('narrow', 'region'))
- weight_grad: float32 [9, 64, 192], replicated
Inputs may be any that keep to these rules, and one draw needn't show every extreme that they name: `point_owner`: among the 4096 points of one device no owner is named more than 256 times, a bound that some block reaches.
All inputs are finite; a program needn't handle non-finite values.
Results may differ from a plain program's by a relative error of at most 0.0036.
Values may be sent and summed in bfloat16 or wider, within the bound.
A program may use at most 192 MiB of HBM per device.

v0:
```python
import math
import jax
import jax.numpy as jnp
from jax import lax
from jax.sharding import PartitionSpec as P

NZ = 64
CY = 8


def extended(cells, sides, width):
    for axis, dim in sides:
        count = lax.axis_size(axis)
        ends = count - 1
        head = lax.slice_in_dim(cells, 0, width, axis=dim)
        tail = lax.slice_in_dim(cells, cells.shape[dim] - width, cells.shape[dim], axis=dim)
        cells = jnp.concatenate(
            [
                lax.ppermute(tail, axis, [(i, (i + 1) % count) for i in range(ends)]),
                cells,
                lax.ppermute(head, axis, [((i + 1) % count, i) for i in range(ends)]),
            ],
            axis=dim,
        )
    return cells


def stack_depth(padded, offsets, depth):
    return jnp.concatenate([padded[..., o : o + depth] for o in offsets], axis=0)


def shards(point_feats, point_owner, point_voxel, weight, cotangent):
    n_narrow = lax.axis_size("narrow")
    n_region = lax.axis_size("region")
    devices = n_narrow * n_region
    chans, points_here = point_feats.shape
    slots = 2 * points_here // devices
    rows_x = cotangent.shape[1]
    voxels = rows_x * CY * NZ
    owner = point_owner[:, 0]
    marks = (owner[:, None] == jnp.arange(devices, dtype=jnp.int32)[None, :]).astype(jnp.int32)
    slot = jnp.sum(jnp.cumsum(marks, axis=0) * marks, axis=1) - 1
    send_feats = jnp.zeros((devices, slots, chans), jnp.bfloat16).at[owner, slot].set(point_feats.T)
    send_feats = send_feats.reshape(devices, slots * chans)
    send_vox = jnp.zeros((devices, slots), jnp.int32).at[owner, slot].set(point_voxel)
    got_feats, got_vox = (
        lax.all_to_all(send_feats, ("narrow", "region"), split_axis=0, concat_axis=0, tiled=True),
        lax.all_to_all(send_vox, ("narrow", "region"), split_axis=0, concat_axis=0, tiled=True),
    )
    incoming = got_feats.reshape(devices * slots, chans).astype(jnp.float32)
    targets = got_vox.reshape(devices * slots)
    sums = jax.ops.segment_sum(incoming, targets, num_segments=voxels)
    grid = sums.T.astype(jnp.bfloat16).reshape(chans, rows_x, CY, NZ)
    grads = cotangent.reshape(chans, rows_x, CY, NZ)
    padded = extended(grid, (("narrow", 2), ("region", 1)), 1)
    gpad = extended(grads, (("narrow", 2), ("region", 1)), 1)
    padded = jnp.pad(padded, ((0, 0), (0, 0), (0, 0), (1, 1)))
    stacked = stack_depth(padded, [0, 1, 2], NZ)
    gpad = jnp.pad(gpad, ((0, 0), (0, 0), (0, 0), (1, 1)))
    gstack = stack_depth(gpad, [2, 1, 0], NZ)
    flipped = weight.reshape(9, chans, 3, chans).transpose(0, 3, 2, 1).reshape(9, chans, 3 * chans)
    result = jnp.zeros((chans, rows_x, CY, NZ), jnp.float32)
    backward = jnp.zeros((chans, rows_x, CY, NZ), jnp.float32)
    kernels = []
    for a in range(3):
        for b in range(3):
            k = a * 3 + b
            window = stacked[:, a : a + rows_x, b : b + CY]
            result = result + jnp.einsum(
                "ok,kxyz->oxyz", weight[k], window, preferred_element_type=jnp.float32
            )
            kernels.append(
                jnp.einsum("oxyz,kxyz->ok", grads, window, preferred_element_type=jnp.float32)
            )
            backward = backward + jnp.einsum(
                "ck,kxyz->cxyz",
                flipped[k],
                gstack[:, 2 - a : 2 - a + rows_x, 2 - b : 2 - b + CY],
                preferred_element_type=jnp.float32,
            )
    conv_out = result.astype(jnp.bfloat16).reshape(chans, rows_x, CY * NZ)
    total_cells = rows_x * n_region * CY * n_narrow * NZ
    weight_grad = lax.psum(jnp.stack(kernels), ("narrow", "region")) * (
        1.0 / math.sqrt(total_cells)
    )
    grad_flat = backward.astype(jnp.bfloat16).reshape(chans, voxels)
    picked = jnp.take(grad_flat, targets, axis=1).T.reshape(devices, slots * chans)
    returned = lax.all_to_all(picked, ("narrow", "region"), split_axis=0, concat_axis=0, tiled=True)
    returned = returned.reshape(devices, slots, chans)
    point_grad = returned[owner, slot].T
    return (conv_out, point_grad, weight_grad)


def solution(mesh):
    in_specs = (
        P(None, ("narrow", "region")),
        P(("narrow", "region"), None),
        P(("narrow", "region")),
        P(),
        P(None, "region", "narrow"),
    )
    out_specs = (P(None, "region", "narrow"), P(None, ("narrow", "region")), P())
    return jax.shard_map(shards, mesh=mesh, in_specs=in_specs, out_specs=out_specs, check_vma=False)
```

profile of v0, /device:TPU:0, one launch (start us, length us, event | category | flops | bytes accessed | tf_op | source)
XLA Modules:
  0.0 687.5 jit_solution(5900122822803206030)
XLA Ops:
  7.9 9.2 %reduce-window.6 = s32[32,32,128]{2,1,0:T(8,128)S(1)} reduce-window(s32[32,32,128]{2,1,0:T(8,128)S(1)} %fusion.21, s32[]{:T(128)} %constant.14.clone.1), window={size=1x1x128 pad=0_0x0_0x127_0}, to_apply=%region_0.0 | reduce-window | flops 16646144 | bytes 1048580 | tf_op jit(solution)/shard_map/reduce-window
  21.8 16.3 %scatter_custom_fusion.1 = s32[8192]{0:T(1024)} fusion(s32[4096]{0:T(1024)S(1)} %broadcast_select_fusion.1, s32[4096]{0:T(1024)} %param.7, s32[]{:T(128)} %constant.14.clone.1), kind=kCustom, calls=%fused_computation.98 | custom fusion | bytes 33280
  38.1 7.4 %all-to-all-start = ((s32[32,1,256]{2,1,0:T(1,128)}), s32[32,1,256]{2,1,0:T(1,128)}, u32[]{:S(2)}, u32[]{:S(2)}) async-start(s32[32,1,256]{2,1,0:T(1,128)} %bitcast.5), calls=%async_computation | async-start | bytes 65536 | tf_op jit(solution)/shard_map/all_to_all | solution.py:48
  45.5 3.4 copy.56
  49.9 3.6 collective-permute-start.4
  58.5 2.4 copy.54
  60.9 12.9 %scatter_custom_fusion.2 = bf16[8192,64]{1,0:T(8,128)(2,1)} fusion(s32[4096]{0:T(1024)} %copy-done.17, bf16[4096,64]{1,0:T(8,128)(2,1)} %copy.54, bf16[]{:T(256)} %constant.33.clone.1), kind=kCustom, calls=%fused_computation.45 | custom fusion | bytes 1049088
  73.8 6.2 all_to_all.24
  80.6 9.4 %reduce.11 = bf16[32,16384]{1,0:T(8,128)(2,1)} reduce(bf16[32,1,16384]{2,1,0:T(2,128)(2,1)} %all_to_all.24, bf16[]{:T(256)} %broadcast.231), dimensions={1}, to_apply=%all_to_all.24.reduce_sub_computation | reduce | bytes 2097154 | tf_op jit(solution)/shard_map/all_to_all | solution.py:47
  89.9 2.6 reshape.224
  106.1 7.6 %all-to-all-start.1 = ((bf16[32,2,8192]{2,1,0:T(2,128)(2,1)}), bf16[32,2,8192]{2,1,0:T(2,128)(2,1)}, u32[]{:S(2)}, u32[]{:S(2)}) async-start(bf16[32,2,8192]{2,1,0:T(2,128)(2,1)} %reshape.224), calls=%async_computation.1 | async-start | bytes 2097152 | tf_op jit(solution)/shard_map/all_to_all | solution.py:47
  122.4 9.0 %select_maximum_fusion = bf16[64,26,10,66]{0,3,2,1:T(8,128)(2,1)S(1)} fusion(bf16[64,1,10,64]{0,3,2,1:T(8,128)(2,1)S(1)} %collective-permute-done.7, bf16[64,1,10,64]{0,3,2,1:T(8,128)(2,1)S(1)} %collective-permute-done.6, bf16[64,24,1,64]{0,3,2,1:T(8,128)(2,1)} %collective-permute-done.5, bf16[64,24,8,64]{0,3,2,1:T(8,128)(2,1)S(1)} %bitcast.265, ...), kind=kLoop, calls=%fused_computation.12 | loop fusion | flops 19768320 | bytes 4326400 | tf_op jit(solution)/shard_map/concatenate | solution.py:17
  131.4 2.4 fusion.50
  133.8 11.6 %pad_maximum_fusion.1 = bf16[192,26,10,64]{0,3,2,1:T(8,128)(2,1)S(1)} fusion(bf16[64,26,10,64]{0,3,2,1:T(8,128)(2,1)S(1)} %get-tuple-element.15, bf16[64,1,10,64]{0,3,2,1:T(8,128)(2,1)S(1)} %collective-permute-done.7, bf16[64,24,1,64]{0,3,2,1:T(8,128)(2,1)} %collective-permute-done.5, bf16[64,24,8,64]{0,3,2,1:T(8,128)(2,1)S(1)} %bitcast.266, ...), kind=kLoop, calls=%fused_computation.9 | loop fusion | flops 44728320 | bytes 12779520 | tf_op jit(solution)/shard_map/concatenate | solution.py:29
  145.4 4.4 fusion.55
  149.8 4.4 fusion.56
  154.3 4.4 fusion.57
  158.7 4.4 fusion.58
  163.0 4.5 fusion.59
  167.5 4.4 fusion.60
  171.9 4.4 fusion.61
  176.3 4.9 fusion.62
  181.2 18.4 %add_convert_fusion = bf16[24,8,64,64]{3,2,1,0:T(8,128)(2,1)} fusion(f32[24,8,64,64]{3,2,1,0:T(8,128)} %fusion.62, f32[24,8,64,64]{3,2,1,0:T(8,128)} %fusion.61, f32[24,8,64,64]{3,2,1,0:T(8,128)} %fusion.60, f32[24,8,64,64]{3,2,1,0:T(8,128)} %fusion.59, f32[24,8,64,64]{3,2,1,0:T(8,128)} %fusion.58, f32[24,8,64,64]{3,2,1,0:T(8,128)} %fusion.57, ...), kind=kOutput, calls=%fused_computation.10 | convolution fusion | flops 309067776 | bytes 33153024 | tf_op jit(solution)/shard_map/ck,kxyz->cxyz/dot_general | solution.py:75
  199.6 30.4 %gather_fusion = bf16[8192,64]{1,0:T(8,128)(2,1)} fusion(bf16[64,12288]{0,1:T(8,128)(2,1)} %bitcast.281, s32[8192]{0:T(1024)S(1)} %copy-done.15), kind=kCustom, calls=%fused_computation | custom fusion | bytes 2129920 | tf_op jit(solution)/shard_map/jit(_take)/gather | solution.py:87
  230.1 6.6 broadcast_select_fusion
  236.6 6.2 all_to_all.25
  242.8 9.4 %reduce.12 = bf16[32,16384]{1,0:T(8,128)(2,1)} reduce(bf16[32,1,16384]{2,1,0:T(2,128)(2,1)} %all_to_all.25, bf16[]{:T(256)} %broadcast.231), dimensions={1}, to_apply=%all_to_all.25.reduce_sub_computation | reduce | bytes 2097154 | tf_op jit(solution)/shard_map/all_to_all | solution.py:88
  252.2 2.6 reshape.226
  254.8 21.9 %all-to-all-start.2 = ((bf16[32,2,8192]{2,1,0:T(2,128)(2,1)}), bf16[32,2,8192]{2,1,0:T(2,128)(2,1)}, u32[]{:S(2)}, u32[]{:S(2)}) async-start(bf16[32,2,8192]{2,1,0:T(2,128)(2,1)} %reshape.226), calls=%async_computation.2 | async-start | bytes 2097152 | tf_op jit(solution)/shard_map/all_to_all | solution.py:88
  276.8 5.9 reshape.225
  282.7 9.0 %convert_reduce_fusion = f32[32,16384]{1,0:T(8,128)} fusion(bf16[32,1,16384]{2,1,0:T(2,128)(2,1)} %reshape.225), kind=kLoop, calls=%fused_computation.25 | loop fusion | flops 524288 | bytes 3145728 | tf_op jit(solution)/shard_map/convert_element_type | solution.py:50
  291.7 4.3 reshape.171
  296.0 52.3 %scatter_custom_fusion = f32[12288,64]{1,0:T(8,128)} fusion(s32[8192]{0:T(1024)} %bitcast.6, f32[8192,64]{1,0:T(8,128)} %reshape.171, f32[]{:T(128)} %constant.13.clone.1), kind=kCustom, calls=%fused_computation.23 | custom fusion | flops 524288 | bytes 3146240 | tf_op jit(solution)/shard_map/scatter-add | solution.py:52
  348.3 3.0 convert_element_type.29
  351.4 8.3 %collective-permute-start = (bf16[64,24,1,64]{0,3,2,1:T(8,128)(2,1)S(1)}, bf16[64,24,1,64]{0,3,2,1:T(8,128)(2,1)S(1)}, u32[]{:S(2)}, u32[]{:S(2)}) collective-permute-start(bf16[64,24,1,64]{0,3,2,1:T(8,128)(2,1)S(1)} %get-tuple-element.24), channel_id=1, source_target_pairs={{0,8},{8,16},{16,24},{1,9},{9,17},{17,25},{2,10},{10,18},{18,26},{... | collective-permute-start | bytes 589832 | tf_op jit(solution)/shard_map/ppermute | solution.py:19
  361.1 4.0 collective-permute-done
  365.0 5.9 collective-permute-done.1
  375.1 6.2 reshape.227
  381.3 8.7 %reduce.6 = bf16[32,16384]{1,0:T(8,128)(2,1)} reduce(bf16[32,1,16384]{2,1,0:T(2,128)(2,1)} %reshape.227, bf16[]{:T(256)} %constant.72), dimensions={1}, to_apply=%all_to_all.23.reduce_sub_computation | reduce | bytes 2097154 | tf_op jit(solution)/shard_map/all_to_all | solution.py:88
  390.0 4.0 reshape.141
  394.0 67.6 %gather_fusion.1 = bf16[4096,64]{1,0:T(8,128)(2,1)} fusion(bf16[32,256,64]{2,1,0:T(8,128)(2,1)} %reshape.141, s32[4096]{0:T(1024)S(1)} %bitcast.276), kind=kCustom, calls=%fused_computation.1 | custom fusion | bytes 1081344 | tf_op jit(solution)/shard_map/gather | solution.py:90
  461.6 2.3 copy.87
  464.0 9.6 %select_maximum_fusion.4 = bf16[64,26,10,66]{0,3,2,1:T(8,128)(2,1)S(1)} fusion(bf16[64,1,10,64]{0,3,2,1:T(8,128)(2,1)} %collective-permute-done.3, bf16[64,1,10,64]{0,3,2,1:T(8,128)(2,1)} %collective-permute-done.2, bf16[64,24,1,64]{0,3,2,1:T(8,128)(2,1)} %copy-done.3, bf16[64,24,8,64]{0,3,2,1:T(8,128)(2,1)} %bitcast.279, ...), kind=kLoop, calls=%fused_computation.16 | loop fusion | flops 19768320 | bytes 4326400 | tf_op jit(solution)/shard_map/concatenate | solution.py:17
  473.6 2.3 fusion.51
  475.9 11.3 %pad_maximum_fusion = bf16[192,26,10,64]{0,3,2,1:T(8,128)(2,1)S(1)} fusion(bf16[64,26,10,64]{0,3,2,1:T(8,128)(2,1)S(1)} %get-tuple-element.17, bf16[64,1,10,64]{0,3,2,1:T(8,128)(2,1)} %collective-permute-done.3, bf16[64,24,1,64]{0,3,2,1:T(8,128)(2,1)S(1)} %copy-done.4, bf16[64,24,8,64]{0,3,2,1:T(8,128)(2,1)S(1)} %bitcast.280, ...), kind=kLoop, calls=%fused_computation.8 | loop fusion | flops 44728320 | bytes 12779520 | tf_op jit(solution)/shard_map/concatenate | solution.py:29
  487.2 2.8 fusion.16
  490.0 4.5 fusion.23
  494.4 4.3 fusion.25
  498.8 4.4 fusion.27
  503.2 4.4 fusion.29
  507.6 4.4 fusion.31
  512.0 4.3 fusion.33
  516.3 4.4 fusion.35
  520.7 4.6 fusion.37
  527.4 2.1 fusion.14
  529.5 2.1 fusion.13
  531.7 2.1 fusion.12
  533.8 2.1 fusion.11
  535.9 2.1 fusion.10
  538.0 2.1 fusion.9
  540.2 2.1 fusion.8
  542.3 18.5 %add_convert_fusion.1 = bf16[24,8,64,64]{3,2,1,0:T(8,128)(2,1)S(1)} fusion(f32[24,8,64,64]{3,2,1,0:T(8,128)} %fusion.23, f32[24,8,64,64]{3,2,1,0:T(8,128)} %fusion.25, f32[24,8,64,64]{3,2,1,0:T(8,128)} %fusion.27, f32[24,8,64,64]{3,2,1,0:T(8,128)} %fusion.29, f32[24,8,64,64]{3,2,1,0:T(8,128)} %fusion.31, f32[24,8,64,64]{3,2,1,0:T(8,128)} %fusion.33, ...), kind=kOutput, calls=%fused_computation.11 | convolution fusion | flops 309067776 | bytes 33161216 | tf_op jit(solution)/shard_map/ok,kxyz->oxyz/dot_general | solution.py:69
  560.8 3.1 copy.86
  564.0 114.5 %all-reduce.4.cloned.1.call-done = f32[9,64,192]{2,1,0:T(8,128)} async-done(((f32[9,64,192]{2,1,0:T(8,128)}), f32[9,64,192]{2,1,0:T(8,128)}) %all-reduce.4.cloned.1.call-update) | async-done | bytes 442384 | tf_op jit(solution)/shard_map/psum | solution.py:83
  (84 shorter events, 43.8 us)
Async XLA Ops:
  21.8 16.3 %copy-start.17 = (s32[4096]{0:T(1024)}, s32[4096]{0:T(1024)S(1)}, u32[]{:S(2)}) copy-start(s32[4096]{0:T(1024)S(1)} %broadcast_select_fusion.1) | copy-start | bytes 49156
  38.1 68.0 %all-to-all-start = ((s32[32,1,256]{2,1,0:T(1,128)}), s32[32,1,256]{2,1,0:T(1,128)}, u32[]{:S(2)}, u32[]{:S(2)}) async-start(s32[32,1,256]{2,1,0:T(1,128)} %bitcast.5), calls=%async_computation | async-start | bytes 65536 | tf_op jit(solution)/shard_map/all_to_all | solution.py:48
  49.9 65.2 %collective-permute-start.4 = (bf16[64,24,1,64]{0,3,2,1:T(8,128)(2,1)}, bf16[64,24,1,64]{0,3,2,1:T(8,128)(2,1)S(1)}, u32[]{:S(2)}, u32[]{:S(2)}) collective-permute-start(bf16[64,24,1,64]{0,3,2,1:T(8,128)(2,1)} %get-tuple-element.22), channel_id=1, source_target_pairs={{0,8},{8,16},{16,24},{1,9},{9,17},{17,25},{2,10},{10,18},{18,26},{... | collective-permute-start | bytes 589832 | tf_op jit(solution)/shard_map/ppermute | solution.py:19
  53.5 61.6 %collective-permute-start.5 = (bf16[64,24,1,64]{0,3,2,1:T(8,128)(2,1)}, bf16[64,24,1,64]{0,3,2,1:T(8,128)(2,1)}, u32[]{:S(2)}, u32[]{:S(2)}) collective-permute-start(bf16[64,24,1,64]{0,3,2,1:T(8,128)(2,1)} %get-tuple-element.23), channel_id=1, source_target_pairs={{8,0},{16,8},{24,16},{9,1},{17,9},{25,17},{10,2},{18,10},{26,18},{... | collective-permute-start | bytes 589832 | tf_op jit(solution)/shard_map/ppermute | solution.py:21
  106.1 148.8 %all-to-all-start.1 = ((bf16[32,2,8192]{2,1,0:T(2,128)(2,1)}), bf16[32,2,8192]{2,1,0:T(2,128)(2,1)}, u32[]{:S(2)}, u32[]{:S(2)}) async-start(bf16[32,2,8192]{2,1,0:T(2,128)(2,1)} %reshape.224), calls=%async_computation.1 | async-start | bytes 2097152 | tf_op jit(solution)/shard_map/all_to_all | solution.py:47
  115.9 4.8 collective-permute-start.6
  118.0 4.4 collective-permute-start.7
  133.7 11.6 %copy-start.7 = (bf16[1,64,3,64]{1,3,2,0:T(8,128)(2,1)S(1)}, bf16[1,64,3,64]{1,3,2,0:T(8,128)(2,1)}, u32[]{:S(2)}) copy-start(bf16[1,64,3,64]{1,3,2,0:T(8,128)(2,1)} %copy.58) | copy-start | bytes 73732
  145.4 4.5 copy-start.8
  149.8 4.4 copy-start.9
  154.3 4.4 copy-start.10
  158.6 4.4 copy-start.11
  163.0 4.5 copy-start.12
  167.5 4.4 copy-start.13
  171.9 4.4 copy-start.14
  176.3 4.9 copy-start.6
  181.2 18.4 %copy-start.15 = (s32[8192]{0:T(1024)S(1)}, s32[8192]{0:T(1024)}, u32[]{:S(2)}) copy-start(s32[8192]{0:T(1024)} %broadcast_clamp_fusion) | copy-start | bytes 98308
  199.6 30.4 %copy-start.16 = (pred[8192]{0:T(1024)(128)(4,1)S(1)}, pred[8192]{0:T(1024)(128)(4,1)}, u32[]{:S(2)}) copy-start(pred[8192]{0:T(1024)(128)(4,1)} %compare_and_fusion) | copy-start | bytes 24580
  254.8 120.2 %all-to-all-start.2 = ((bf16[32,2,8192]{2,1,0:T(2,128)(2,1)}), bf16[32,2,8192]{2,1,0:T(2,128)(2,1)}, u32[]{:S(2)}, u32[]{:S(2)}) async-start(bf16[32,2,8192]{2,1,0:T(2,128)(2,1)} %reshape.226), calls=%async_computation.2 | async-start | bytes 2097152 | tf_op jit(solution)/shard_map/all_to_all | solution.py:88
  276.8 401.7 %all-reduce.4.cloned.1.call-start = ((), (), s32[]{:S(2)}) async-start(), calls=%async_computation.3 | async-start | bytes 1179648 | tf_op jit(solution)/shard_map/psum | solution.py:83
  351.4 19.6 %copy-start.1 = (bf16[12288,64]{1,0:T(8,128)(2,1)}, bf16[12288,64]{1,0:T(8,128)(2,1)S(1)}, u32[]{:S(2)}) copy-start(bf16[12288,64]{1,0:T(8,128)(2,1)S(1)} %convert_element_type.29) | copy-start | bytes 4718596
  351.4 13.6 %collective-permute-start = (bf16[64,24,1,64]{0,3,2,1:T(8,128)(2,1)S(1)}, bf16[64,24,1,64]{0,3,2,1:T(8,128)(2,1)S(1)}, u32[]{:S(2)}, u32[]{:S(2)}) collective-permute-start(bf16[64,24,1,64]{0,3,2,1:T(8,128)(2,1)S(1)} %get-tuple-element.24), channel_id=1, source_target_pairs={{0,8},{8,16},{16,24},{1,9},{9,17},{17,25},{2,10},{10,18},{18,26},{... | collective-permute-start | bytes 589832 | tf_op jit(solution)/shard_map/ppermute | solution.py:19
  359.8 11.2 %collective-permute-start.1 = (bf16[64,24,1,64]{0,3,2,1:T(8,128)(2,1)S(1)}, bf16[64,24,1,64]{0,3,2,1:T(8,128)(2,1)S(1)}, u32[]{:S(2)}, u32[]{:S(2)}) collective-permute-start(bf16[64,24,1,64]{0,3,2,1:T(8,128)(2,1)S(1)} %get-tuple-element.25), channel_id=1, source_target_pairs={{8,0},{16,8},{24,16},{9,1},{17,9},{25,17},{10,2},{18,10},{26,18},{... | collective-permute-start | bytes 589832 | tf_op jit(solution)/shard_map/ppermute | solution.py:21
  370.9 0.9 copy-start.3
  371.8 92.2 %collective-permute-start.2 = (bf16[64,1,10,64]{0,3,2,1:T(8,128)(2,1)}, bf16[64,1,10,64]{0,3,2,1:T(8,128)(2,1)}, u32[]{:S(2)}, u32[]{:S(2)}) collective-permute-start(bf16[64,1,10,64]{0,3,2,1:T(8,128)(2,1)} %get-tuple-element.20), channel_id=1, source_target_pairs={{0,1},{1,2},{2,3},{3,4},{4,5},{5,6},{6,7},{8,9},{9,10},{10,11},{11... | collective-permute-start | bytes 245768 | tf_op jit(solution)/shard_map/ppermute | solution.py:19
  373.8 90.2 %collective-permute-start.3 = (bf16[64,1,10,64]{0,3,2,1:T(8,128)(2,1)}, bf16[64,1,10,64]{0,3,2,1:T(8,128)(2,1)}, u32[]{:S(2)}, u32[]{:S(2)}) collective-permute-start(bf16[64,1,10,64]{0,3,2,1:T(8,128)(2,1)} %get-tuple-element.21), channel_id=1, source_target_pairs={{1,0},{2,1},{3,2},{4,3},{5,4},{6,5},{7,6},{9,8},{10,9},{11,10},{12... | collective-permute-start | bytes 245768 | tf_op jit(solution)/shard_map/ppermute | solution.py:21
  473.5 2.4 copy-start.2
  473.6 2.4 copy-start.4
  487.2 53.0 %copy-start = (bf16[192,26,10,64]{0,3,2,1:T(8,128)(2,1)}, bf16[192,26,10,64]{0,3,2,1:T(8,128)(2,1)S(1)}, u32[]{:S(2)}) copy-start(bf16[192,26,10,64]{0,3,2,1:T(8,128)(2,1)S(1)} %pad_maximum_fusion) | copy-start | bytes 19169284
  487.2 2.8 copy-start.5
Sparse Core Ops, SparseCore 0:
  542.4 135.9 all-reduce.3
where the time goes:
time: 696 us; the launch traced here: 687 us
  local copies, waits for them, and re-layouts  201 us (29%)
  other arithmetic  160 us (23%)
  matrix products  128 us (18%)
  waiting for transfers between devices  126 us (18%)
  starting transfers between devices  58.1 us (8%)
  between operations  14.6 us (2%)
    psum x1, waiting for transfers between devices, shards(): lax.psum(jnp.stack(kernels), ('narrow', 'region'))  114 us
    gather x1, local copies, waits for them, and re-layouts, shards(): point_grad = returned[owner, slot].T  67.6 us
    unnamed x46, local copies, waits for them, and re-layouts  57.5 us
    dot_general x9, matrix products, shards(): jnp.einsum('ck,kxyz->cxyz', flipped[k], gstack[:, 2 - a:2 - a + rows_x, 2...  54.2 us
    dot_general x9, matrix products, shards(): jnp.einsum('ok,kxyz->oxyz', weight[k], window, preferred_element_type=jnp...  53.8 us
    scatter-add x1, other arithmetic, shards(): sums = jax.ops.segment_sum(incoming, targets, num_segments=voxels)  52.3 us
    gather x1, local copies, waits for them, and re-layouts, shards(): jnp.take(grad_flat, targets, axis=1).T.reshape(devices, slots * chans)  30.4 us
    concatenate x2, other arithmetic, stack_depth(): return jnp.concatenate([padded[..., o:o + depth] for o in offsets], axis=0)  22.9 us
  transfers between devices with their start and end apart: 12, of which 4 were waited for; matrix products, arithmetic and copies ran while one was open for 53% of the time, Pallas kernels for 0%

commit v1 on v0

--- a/solution.py
+++ b/solution.py
@@ -1,3 +1,4 @@
+import functools
 import math
 import jax
 import jax.numpy as jnp
@@ -6,6 +7,15 @@
 
 NZ = 64
 CY = 8
+
+
+def _map_shifts_all(array_in, axis_tag, shard_axis):
+    for dev in (axis_tag, shard_axis):
+        array_in = lax.psum(array_in, dev)
+    return array_in
+
+
+write_tracks_now = functools.partial(_map_shifts_all, axis_tag="region", shard_axis="narrow")
 
 
 def extended(cells, sides, width):
@@ -80,9 +90,7 @@
             )
     conv_out = result.astype(jnp.bfloat16).reshape(chans, rows_x, CY * NZ)
     total_cells = rows_x * n_region * CY * n_narrow * NZ
-    weight_grad = lax.psum(jnp.stack(kernels), ("narrow", "region")) * (
-        1.0 / math.sqrt(total_cells)
-    )
+    weight_grad = write_tracks_now(jnp.stack(kernels)) * (1.0 / math.sqrt(total_cells))
     grad_flat = backward.astype(jnp.bfloat16).reshape(chans, voxels)
     picked = jnp.take(grad_flat, targets, axis=1).T.reshape(devices, slots * chans)
     returned = lax.all_to_all(picked, ("narrow", "region"), split_axis=0, concat_axis=0, tiled=True)

time: 696 us -> 669 us (0.961)
  waiting for transfers between devices: 126 us -> 96.2 us
    psum x1 -> x2, waiting for transfers between devices: 114 us -> 84.6 us  [_map_shifts_all(): array_in = lax.psum(array_in, dev)]
  transfers between devices with their start and end apart: 12 -> 13, of which waited for: 4 -> 5; matrix products, arithmetic and copies ran while one was open for 53% -> 56% of each run, Pallas kernels for 0% -> 0%
where the time goes in v1:
time: 669 us; the launch traced here: 661 us
  local copies, waits for them, and re-layouts  201 us (30%)
  other arithmetic  160 us (24%)
  matrix products  131 us (20%)
  waiting for transfers between devices  96.2 us (14%)
  starting transfers between devices  58.2 us (9%)
  between operations  14.6 us (2%)
    psum x2, waiting for transfers between devices, _map_shifts_all(): array_in = lax.psum(array_in, dev)  84.6 us
    gather x1, local copies, waits for them, and re-layouts, shards(): point_grad = returned[owner, slot].T  67.6 us
    unnamed x46, local copies, waits for them, and re-layouts  57.5 us
    dot_general x9, matrix products, shards(): jnp.einsum('ok,kxyz->oxyz', weight[k], window, preferred_element_type=jnp...  56.6 us
    dot_general x9, matrix products, shards(): jnp.einsum('ck,kxyz->cxyz', flipped[k], gstack[:, 2 - a:2 - a + rows_x, 2...  54.2 us
    scatter-add x1, other arithmetic, shards(): sums = jax.ops.segment_sum(incoming, targets, num_segments=voxels)  52.3 us
    gather x1, local copies, waits for them, and re-layouts, shards(): jnp.take(grad_flat, targets, axis=1).T.reshape(devices, slots * chans)  30.4 us
    concatenate x2, other arithmetic, stack_depth(): return jnp.concatenate([padded[..., o:o + depth] for o in offsets], axis=0)  22.9 us
  transfers between devices with their start and end apart: 13, of which 5 were waited for; matrix products, arithmetic and copies ran while one was open for 56% of the time, Pallas kernels for 0%

profile of v1, /device:TPU:0, one launch (start us, length us, event | category | flops | bytes accessed | tf_op | source)
XLA Modules:
  0.0 660.6 jit_solution(17439571040194345483)
XLA Ops:
  7.9 9.2 %reduce-window.6 = s32[32,32,128]{2,1,0:T(8,128)S(1)} reduce-window(s32[32,32,128]{2,1,0:T(8,128)S(1)} %fusion.21, s32[]{:T(128)} %constant.14.clone.1), window={size=1x1x128 pad=0_0x0_0x127_0}, to_apply=%region_0.0 | reduce-window | flops 16646144 | bytes 1048580 | tf_op jit(solution)/shard_map/reduce-window
  21.8 16.3 %scatter_custom_fusion.1 = s32[8192]{0:T(1024)} fusion(s32[4096]{0:T(1024)S(1)} %broadcast_select_fusion.1, s32[4096]{0:T(1024)} %param.7, s32[]{:T(128)} %constant.14.clone.1), kind=kCustom, calls=%fused_computation.98 | custom fusion | bytes 33280
  38.1 7.4 %all-to-all-start = ((s32[32,1,256]{2,1,0:T(1,128)}), s32[32,1,256]{2,1,0:T(1,128)}, u32[]{:S(2)}, u32[]{:S(2)}) async-start(s32[32,1,256]{2,1,0:T(1,128)} %bitcast.5), calls=%async_computation | async-start | bytes 65536 | tf_op jit(solution)/shard_map/all_to_all | solution.py:58
  45.5 3.4 copy.56
  49.9 3.6 collective-permute-start.4
  58.5 2.4 copy.54
  60.9 12.9 %scatter_custom_fusion.2 = bf16[8192,64]{1,0:T(8,128)(2,1)} fusion(s32[4096]{0:T(1024)} %copy-done.17, bf16[4096,64]{1,0:T(8,128)(2,1)} %copy.54, bf16[]{:T(256)} %constant.33.clone.1), kind=kCustom, calls=%fused_computation.45 | custom fusion | bytes 1049088
  73.8 6.2 all_to_all.24
  80.6 9.4 %reduce.11 = bf16[32,16384]{1,0:T(8,128)(2,1)} reduce(bf16[32,1,16384]{2,1,0:T(2,128)(2,1)} %all_to_all.24, bf16[]{:T(256)} %broadcast.231), dimensions={1}, to_apply=%all_to_all.24.reduce_sub_computation | reduce | bytes 2097154 | tf_op jit(solution)/shard_map/all_to_all | solution.py:57
  89.9 2.6 reshape.224
  106.1 7.6 %all-to-all-start.1 = ((bf16[32,2,8192]{2,1,0:T(2,128)(2,1)}), bf16[32,2,8192]{2,1,0:T(2,128)(2,1)}, u32[]{:S(2)}, u32[]{:S(2)}) async-start(bf16[32,2,8192]{2,1,0:T(2,128)(2,1)} %reshape.224), calls=%async_computation.1 | async-start | bytes 2097152 | tf_op jit(solution)/shard_map/all_to_all | solution.py:57
  122.4 9.0 %select_maximum_fusion = bf16[64,26,10,66]{0,3,2,1:T(8,128)(2,1)S(1)} fusion(bf16[64,1,10,64]{0,3,2,1:T(8,128)(2,1)S(1)} %collective-permute-done.7, bf16[64,1,10,64]{0,3,2,1:T(8,128)(2,1)S(1)} %collective-permute-done.6, bf16[64,24,1,64]{0,3,2,1:T(8,128)(2,1)} %collective-permute-done.5, bf16[64,24,8,64]{0,3,2,1:T(8,128)(2,1)S(1)} %bitcast.265, ...), kind=kLoop, calls=%fused_computation.12 | loop fusion | flops 19768320 | bytes 4326400 | tf_op jit(solution)/shard_map/concatenate | solution.py:27
  131.4 2.4 fusion.50
  133.8 11.6 %pad_maximum_fusion.1 = bf16[192,26,10,64]{0,3,2,1:T(8,128)(2,1)S(1)} fusion(bf16[64,26,10,64]{0,3,2,1:T(8,128)(2,1)S(1)} %get-tuple-element.15, bf16[64,1,10,64]{0,3,2,1:T(8,128)(2,1)S(1)} %collective-permute-done.7, bf16[64,24,1,64]{0,3,2,1:T(8,128)(2,1)} %collective-permute-done.5, bf16[64,24,8,64]{0,3,2,1:T(8,128)(2,1)S(1)} %bitcast.266, ...), kind=kLoop, calls=%fused_computation.9 | loop fusion | flops 44728320 | bytes 12779520 | tf_op jit(solution)/shard_map/concatenate | solution.py:39
  145.4 4.4 fusion.55
  149.8 4.4 fusion.56
  154.3 4.4 fusion.57
  158.7 4.4 fusion.58
  163.0 4.5 fusion.59
  167.5 4.4 fusion.60
  171.9 4.4 fusion.61
  176.3 4.9 fusion.62
  181.2 18.4 %add_convert_fusion = bf16[24,8,64,64]{3,2,1,0:T(8,128)(2,1)} fusion(f32[24,8,64,64]{3,2,1,0:T(8,128)} %fusion.62, f32[24,8,64,64]{3,2,1,0:T(8,128)} %fusion.61, f32[24,8,64,64]{3,2,1,0:T(8,128)} %fusion.60, f32[24,8,64,64]{3,2,1,0:T(8,128)} %fusion.59, f32[24,8,64,64]{3,2,1,0:T(8,128)} %fusion.58, f32[24,8,64,64]{3,2,1,0:T(8,128)} %fusion.57, ...), kind=kOutput, calls=%fused_computation.10 | convolution fusion | flops 309067776 | bytes 33153024 | tf_op jit(solution)/shard_map/ck,kxyz->cxyz/dot_general | solution.py:85
  199.6 30.4 %gather_fusion = bf16[8192,64]{1,0:T(8,128)(2,1)} fusion(bf16[64,12288]{0,1:T(8,128)(2,1)} %bitcast.281, s32[8192]{0:T(1024)S(1)} %copy-done.15), kind=kCustom, calls=%fused_computation | custom fusion | bytes 2129920 | tf_op jit(solution)/shard_map/jit(_take)/gather | solution.py:95
  230.1 6.6 broadcast_select_fusion
  236.6 6.2 all_to_all.25
  242.8 9.4 %reduce.12 = bf16[32,16384]{1,0:T(8,128)(2,1)} reduce(bf16[32,1,16384]{2,1,0:T(2,128)(2,1)} %all_to_all.25, bf16[]{:T(256)} %broadcast.231), dimensions={1}, to_apply=%all_to_all.25.reduce_sub_computation | reduce | bytes 2097154 | tf_op jit(solution)/shard_map/all_to_all | solution.py:96
  252.2 2.6 reshape.226
  254.8 21.9 %all-to-all-start.2 = ((bf16[32,2,8192]{2,1,0:T(2,128)(2,1)}), bf16[32,2,8192]{2,1,0:T(2,128)(2,1)}, u32[]{:S(2)}, u32[]{:S(2)}) async-start(bf16[32,2,8192]{2,1,0:T(2,128)(2,1)} %reshape.226), calls=%async_computation.2 | async-start | bytes 2097152 | tf_op jit(solution)/shard_map/all_to_all | solution.py:96
  276.8 5.9 reshape.225
  282.7 9.0 %convert_reduce_fusion = f32[32,16384]{1,0:T(8,128)} fusion(bf16[32,1,16384]{2,1,0:T(2,128)(2,1)} %reshape.225), kind=kLoop, calls=%fused_computation.25 | loop fusion | flops 524288 | bytes 3145728 | tf_op jit(solution)/shard_map/convert_element_type | solution.py:60
  291.7 4.3 reshape.171
  296.0 52.3 %scatter_custom_fusion = f32[12288,64]{1,0:T(8,128)} fusion(s32[8192]{0:T(1024)} %bitcast.6, f32[8192,64]{1,0:T(8,128)} %reshape.171, f32[]{:T(128)} %constant.13.clone.1), kind=kCustom, calls=%fused_computation.23 | custom fusion | flops 524288 | bytes 3146240 | tf_op jit(solution)/shard_map/scatter-add | solution.py:62
  348.3 3.0 convert_element_type.29
  351.4 8.3 %collective-permute-start = (bf16[64,24,1,64]{0,3,2,1:T(8,128)(2,1)S(1)}, bf16[64,24,1,64]{0,3,2,1:T(8,128)(2,1)S(1)}, u32[]{:S(2)}, u32[]{:S(2)}) collective-permute-start(bf16[64,24,1,64]{0,3,2,1:T(8,128)(2,1)S(1)} %get-tuple-element.24), channel_id=1, source_target_pairs={{0,8},{8,16},{16,24},{1,9},{9,17},{17,25},{2,10},{10,18},{18,26},{... | collective-permute-start | bytes 589832 | tf_op jit(solution)/shard_map/ppermute | solution.py:29
  361.1 4.0 collective-permute-done
  365.0 5.9 collective-permute-done.1
  375.1 6.2 reshape.227
  381.3 8.7 %reduce.6 = bf16[32,16384]{1,0:T(8,128)(2,1)} reduce(bf16[32,1,16384]{2,1,0:T(2,128)(2,1)} %reshape.227, bf16[]{:T(256)} %constant.72), dimensions={1}, to_apply=%all_to_all.23.reduce_sub_computation | reduce | bytes 2097154 | tf_op jit(solution)/shard_map/all_to_all | solution.py:96
  390.0 4.0 reshape.141
  394.0 67.6 %gather_fusion.1 = bf16[4096,64]{1,0:T(8,128)(2,1)} fusion(bf16[32,256,64]{2,1,0:T(8,128)(2,1)} %reshape.141, s32[4096]{0:T(1024)S(1)} %bitcast.276), kind=kCustom, calls=%fused_computation.1 | custom fusion | bytes 1081344 | tf_op jit(solution)/shard_map/gather | solution.py:98
  461.6 2.3 copy.87
  464.0 9.6 %select_maximum_fusion.4 = bf16[64,26,10,66]{0,3,2,1:T(8,128)(2,1)S(1)} fusion(bf16[64,1,10,64]{0,3,2,1:T(8,128)(2,1)} %collective-permute-done.3, bf16[64,1,10,64]{0,3,2,1:T(8,128)(2,1)} %collective-permute-done.2, bf16[64,24,1,64]{0,3,2,1:T(8,128)(2,1)} %copy-done.3, bf16[64,24,8,64]{0,3,2,1:T(8,128)(2,1)} %bitcast.279, ...), kind=kLoop, calls=%fused_computation.16 | loop fusion | flops 19768320 | bytes 4326400 | tf_op jit(solution)/shard_map/concatenate | solution.py:27
  473.6 2.3 fusion.51
  475.9 11.3 %pad_maximum_fusion = bf16[192,26,10,64]{0,3,2,1:T(8,128)(2,1)S(1)} fusion(bf16[64,26,10,64]{0,3,2,1:T(8,128)(2,1)S(1)} %get-tuple-element.17, bf16[64,1,10,64]{0,3,2,1:T(8,128)(2,1)} %collective-permute-done.3, bf16[64,24,1,64]{0,3,2,1:T(8,128)(2,1)S(1)} %copy-done.4, bf16[64,24,8,64]{0,3,2,1:T(8,128)(2,1)S(1)} %bitcast.280, ...), kind=kLoop, calls=%fused_computation.8 | loop fusion | flops 44728320 | bytes 12779520 | tf_op jit(solution)/shard_map/concatenate | solution.py:39
  487.2 2.8 fusion.16
  490.0 4.5 fusion.23
  494.4 4.3 fusion.25
  498.8 4.4 fusion.27
  503.2 4.4 fusion.29
  507.6 4.4 fusion.31
  512.0 4.3 fusion.33
  516.3 4.4 fusion.35
  520.7 2.1 fusion.15
  522.8 2.3 fusion.14
  527.3 2.1 fusion.12
  529.4 2.1 fusion.11
  533.7 2.1 fusion.9
  535.8 2.1 fusion.8
  538.0 7.2 %fusion.37 = f32[24,8,64,64]{3,2,1,0:T(8,128)} fusion(bf16[192,26,10,64]{0,3,2,1:T(8,128)(2,1)} %copy-done, bf16[9,64,192]{2,1,0:T(8,128)(2,1)S(1)} %copy-done.5), kind=kOutput, calls=%fused_computation.83 | convolution fusion | flops 301989888 | bytes 9568256 | tf_op jit(solution)/shard_map/ok,kxyz->oxyz/dot_general | solution.py:79
  545.2 58.3 %all-reduce.5.cloned.1.call-done = f32[9,64,192]{2,1,0:T(8,128)} async-done(((f32[9,64,192]{2,1,0:T(8,128)}), f32[9,64,192]{2,1,0:T(8,128)}) %all-reduce.5.cloned.1.call-update) | async-done | bytes 442384 | tf_op jit(solution)/shard_map/psum | solution.py:14
  603.5 18.7 %add_convert_fusion.1 = bf16[24,8,64,64]{3,2,1,0:T(8,128)(2,1)S(1)} fusion(f32[24,8,64,64]{3,2,1,0:T(8,128)} %fusion.23, f32[24,8,64,64]{3,2,1,0:T(8,128)} %fusion.25, f32[24,8,64,64]{3,2,1,0:T(8,128)} %fusion.27, f32[24,8,64,64]{3,2,1,0:T(8,128)} %fusion.29, f32[24,8,64,64]{3,2,1,0:T(8,128)} %fusion.31, f32[24,8,64,64]{3,2,1,0:T(8,128)} %fusion.33, ...), kind=kOutput, calls=%fused_computation.11 | convolution fusion | flops 309067776 | bytes 33161216 | tf_op jit(solution)/shard_map/ok,kxyz->oxyz/dot_general | solution.py:79
  622.3 3.1 copy.86
  625.4 26.2 %all-reduce.7.cloned.1.call-done = f32[9,64,192]{2,1,0:T(8,128)} async-done(((f32[9,64,192]{2,1,0:T(8,128)}), f32[9,64,192]{2,1,0:T(8,128)}) %all-reduce.7.cloned.1.call-update) | async-done | bytes 442384 | tf_op jit(solution)/shard_map/psum | solution.py:14
  (87 shorter events, 46.0 us)
Async XLA Ops:
  21.8 16.3 %copy-start.17 = (s32[4096]{0:T(1024)}, s32[4096]{0:T(1024)S(1)}, u32[]{:S(2)}) copy-start(s32[4096]{0:T(1024)S(1)} %broadcast_select_fusion.1) | copy-start | bytes 49156
  38.1 68.0 %all-to-all-start = ((s32[32,1,256]{2,1,0:T(1,128)}), s32[32,1,256]{2,1,0:T(1,128)}, u32[]{:S(2)}, u32[]{:S(2)}) async-start(s32[32,1,256]{2,1,0:T(1,128)} %bitcast.5), calls=%async_computation | async-start | bytes 65536 | tf_op jit(solution)/shard_map/all_to_all | solution.py:58
  49.9 65.2 %collective-permute-start.4 = (bf16[64,24,1,64]{0,3,2,1:T(8,128)(2,1)}, bf16[64,24,1,64]{0,3,2,1:T(8,128)(2,1)S(1)}, u32[]{:S(2)}, u32[]{:S(2)}) collective-permute-start(bf16[64,24,1,64]{0,3,2,1:T(8,128)(2,1)} %get-tuple-element.22), channel_id=1, source_target_pairs={{0,8},{8,16},{16,24},{1,9},{9,17},{17,25},{2,10},{10,18},{18,26},{... | collective-permute-start | bytes 589832 | tf_op jit(solution)/shard_map/ppermute | solution.py:29
  53.5 61.6 %collective-permute-start.5 = (bf16[64,24,1,64]{0,3,2,1:T(8,128)(2,1)}, bf16[64,24,1,64]{0,3,2,1:T(8,128)(2,1)}, u32[]{:S(2)}, u32[]{:S(2)}) collective-permute-start(bf16[64,24,1,64]{0,3,2,1:T(8,128)(2,1)} %get-tuple-element.23), channel_id=1, source_target_pairs={{8,0},{16,8},{24,16},{9,1},{17,9},{25,17},{10,2},{18,10},{26,18},{... | collective-permute-start | bytes 589832 | tf_op jit(solution)/shard_map/ppermute | solution.py:31
  106.1 148.8 %all-to-all-start.1 = ((bf16[32,2,8192]{2,1,0:T(2,128)(2,1)}), bf16[32,2,8192]{2,1,0:T(2,128)(2,1)}, u32[]{:S(2)}, u32[]{:S(2)}) async-start(bf16[32,2,8192]{2,1,0:T(2,128)(2,1)} %reshape.224), calls=%async_computation.1 | async-start | bytes 2097152 | tf_op jit(solution)/shard_map/all_to_all | solution.py:57
  115.9 4.8 collective-permute-start.6
  118.0 4.4 collective-permute-start.7
  133.7 11.6 %copy-start.7 = (bf16[1,64,3,64]{1,3,2,0:T(8,128)(2,1)S(1)}, bf16[1,64,3,64]{1,3,2,0:T(8,128)(2,1)}, u32[]{:S(2)}) copy-start(bf16[1,64,3,64]{1,3,2,0:T(8,128)(2,1)} %copy.58) | copy-start | bytes 73732
  145.4 4.5 copy-start.8
  149.8 4.4 copy-start.9
  154.3 4.4 copy-start.10
  158.6 4.4 copy-start.11
  163.0 4.5 copy-start.12
  167.5 4.4 copy-start.13
  171.9 4.4 copy-start.14
  176.3 4.9 copy-start.6
  181.2 18.4 %copy-start.15 = (s32[8192]{0:T(1024)S(1)}, s32[8192]{0:T(1024)}, u32[]{:S(2)}) copy-start(s32[8192]{0:T(1024)} %broadcast_clamp_fusion) | copy-start | bytes 98308
  199.6 30.4 %copy-start.16 = (pred[8192]{0:T(1024)(128)(4,1)S(1)}, pred[8192]{0:T(1024)(128)(4,1)}, u32[]{:S(2)}) copy-start(pred[8192]{0:T(1024)(128)(4,1)} %compare_and_fusion) | copy-start | bytes 24580
  254.8 120.2 %all-to-all-start.2 = ((bf16[32,2,8192]{2,1,0:T(2,128)(2,1)}), bf16[32,2,8192]{2,1,0:T(2,128)(2,1)}, u32[]{:S(2)}, u32[]{:S(2)}) async-start(bf16[32,2,8192]{2,1,0:T(2,128)(2,1)} %reshape.226), calls=%async_computation.2 | async-start | bytes 2097152 | tf_op jit(solution)/shard_map/all_to_all | solution.py:96
  276.8 326.7 %all-reduce.5.cloned.1.call-start = ((), (), s32[]{:S(2)}) async-start(), calls=%async_computation.3 | async-start | bytes 1179648 | tf_op jit(solution)/shard_map/psum | solution.py:14
  351.4 19.6 %copy-start.1 = (bf16[12288,64]{1,0:T(8,128)(2,1)}, bf16[12288,64]{1,0:T(8,128)(2,1)S(1)}, u32[]{:S(2)}) copy-start(bf16[12288,64]{1,0:T(8,128)(2,1)S(1)} %convert_element_type.29) | copy-start | bytes 4718596
  351.4 13.6 %collective-permute-start = (bf16[64,24,1,64]{0,3,2,1:T(8,128)(2,1)S(1)}, bf16[64,24,1,64]{0,3,2,1:T(8,128)(2,1)S(1)}, u32[]{:S(2)}, u32[]{:S(2)}) collective-permute-start(bf16[64,24,1,64]{0,3,2,1:T(8,128)(2,1)S(1)} %get-tuple-element.24), channel_id=1, source_target_pairs={{0,8},{8,16},{16,24},{1,9},{9,17},{17,25},{2,10},{10,18},{18,26},{... | collective-permute-start | bytes 589832 | tf_op jit(solution)/shard_map/ppermute | solution.py:29
  359.8 11.2 %collective-permute-start.1 = (bf16[64,24,1,64]{0,3,2,1:T(8,128)(2,1)S(1)}, bf16[64,24,1,64]{0,3,2,1:T(8,128)(2,1)S(1)}, u32[]{:S(2)}, u32[]{:S(2)}) collective-permute-start(bf16[64,24,1,64]{0,3,2,1:T(8,128)(2,1)S(1)} %get-tuple-element.25), channel_id=1, source_target_pairs={{8,0},{16,8},{24,16},{9,1},{17,9},{25,17},{10,2},{18,10},{26,18},{... | collective-permute-start | bytes 589832 | tf_op jit(solution)/shard_map/ppermute | solution.py:31
  370.9 0.9 copy-start.3
  371.8 92.2 %collective-permute-start.2 = (bf16[64,1,10,64]{0,3,2,1:T(8,128)(2,1)}, bf16[64,1,10,64]{0,3,2,1:T(8,128)(2,1)}, u32[]{:S(2)}, u32[]{:S(2)}) collective-permute-start(bf16[64,1,10,64]{0,3,2,1:T(8,128)(2,1)} %get-tuple-element.20), channel_id=1, source_target_pairs={{0,1},{1,2},{2,3},{3,4},{4,5},{5,6},{6,7},{8,9},{9,10},{10,11},{11... | collective-permute-start | bytes 245768 | tf_op jit(solution)/shard_map/ppermute | solution.py:29
  373.8 90.2 %collective-permute-start.3 = (bf16[64,1,10,64]{0,3,2,1:T(8,128)(2,1)}, bf16[64,1,10,64]{0,3,2,1:T(8,128)(2,1)}, u32[]{:S(2)}, u32[]{:S(2)}) collective-permute-start(bf16[64,1,10,64]{0,3,2,1:T(8,128)(2,1)} %get-tuple-element.21), channel_id=1, source_target_pairs={{1,0},{2,1},{3,2},{4,3},{5,4},{6,5},{7,6},{9,8},{10,9},{11,10},{12... | collective-permute-start | bytes 245768 | tf_op jit(solution)/shard_map/ppermute | solution.py:31
  473.5 2.4 copy-start.2
  473.6 2.4 copy-start.4
  487.2 48.6 %copy-start = (bf16[192,26,10,64]{0,3,2,1:T(8,128)(2,1)}, bf16[192,26,10,64]{0,3,2,1:T(8,128)(2,1)S(1)}, u32[]{:S(2)}) copy-start(bf16[192,26,10,64]{0,3,2,1:T(8,128)(2,1)S(1)} %pad_maximum_fusion) | copy-start | bytes 19169284
  487.2 2.8 copy-start.5
  538.0 113.7 %all-reduce.7.cloned.1.call-start = ((), (), s32[]{:S(2)}) async-start(), calls=%async_computation.4 | async-start | bytes 1179648 | tf_op jit(solution)/shard_map/psum | solution.py:14
Sparse Core Ops, SparseCore 0:
  538.1 65.3 all-reduce.4
  606.5 45.0 all-reduce.6
